TPU v7x, 32 devices: a whole 2x2x4 slice. The times are simulated.
32 devices in a mesh: block: 8 (over y, x, core), sub: 4 (over z).
Axes of the slice: x: 2, y: 2, z: 4, core: 2. Of those that a mesh axis runs over, the one named last changes fastest.
Arguments:
- source: float32 [8, 16, 128, 128], P('block', 'sub'), may hold values from -48 to 48
- trans_x: float32 [8, 16, 128, 128], P('block', 'sub'), may hold values from 0.1 to 10
- trans_y: float32 [8, 16, 128, 128], P('block', 'sub'), may hold values from 0.1 to 10
- trans_z: float32 [8, 16, 128, 128], P('block', 'sub'), may hold values from 0.1 to 10
- mortar_bot: float32 [8, 16, 128, 256], P('block', 'sub'), may hold values from -0.375 to 0.375
- mortar_top: float32 [8, 16, 128, 256], P('block', 'sub'), may hold values from -0.375 to 0.375
Outputs:
- pressure: float32 [8, 16, 128, 128], P('block', 'sub')
- mortar: float32 [8, 256], P('block', 'sub')
All inputs are finite; a program needn't handle non-finite values.
Results may differ from a plain program's by a relative error of at most 0.0003.
Values sent between devices are 32-bit elements; how exact they have to be, the bound alone decides.
No kernel may reach another device: no remote copies, remote signals or barrier semaphores. Data moves between devices by JAX's collectives and lax.ppermute only.
A program may use at most 64 MiB of HBM per device.

v0:
```python
import jax
import jax.numpy as jnp
from jax import lax
from jax.sharding import PartitionSpec as P

PASSES = 3
OUTER = 2


RELAX = 0.8
MORTAR_STEP = 0.05
HIGHEST = lax.Precision.HIGHEST


def from_behind(block, axis, distance):
    devices = range(lax.axis_size(axis))
    route = [(i - distance, i) for i in devices if i - distance in devices]
    return lax.ppermute(block, axis, route)


def with_halo(value, sides, width):
    for axis, dim in sides:
        devices, length = (lax.axis_size(axis), value.shape[dim])
        up = [(i, (i + 1) % devices) for i in range(devices - 1)]
        down = [(j, i) for i, j in up]
        last = lax.slice_in_dim(value, length - width, length, axis=dim)
        leading = lax.slice_in_dim(value, 0, width, axis=dim)
        before = lax.ppermute(last, axis, up)
        after = lax.ppermute(leading, axis, down)
        value = jnp.concatenate([before, value, after], axis=dim)
    return value


def below_of(values, axis):
    widths = [(0, 0)] * values.ndim
    widths[axis] = (1, 0)
    return lax.slice_in_dim(jnp.pad(values, widths), 0, values.shape[axis], axis=axis)


def above_of(values, axis):
    widths = [(0, 0)] * values.ndim
    widths[axis] = (0, 1)
    return lax.slice_in_dim(jnp.pad(values, widths), 1, values.shape[axis] + 1, axis=axis)


def widen_one(values):
    return jnp.pad(values, ((0, 0), (1, 1), (0, 0), (0, 0)))


def relax_pass(padded, rhs_part, offset, coeffs):
    coupling_x, coupling_next, coupling_y, coupling_z, diagonal = coeffs
    count = padded.shape[1] - 2

    def window(values):
        return values[:, offset : offset + count]

    centre = padded[:, 1:-1]
    part_x = window(coupling_x)
    part_next = window(coupling_next)
    part_y = window(coupling_y)
    part_z = window(coupling_z)
    part_diag = window(diagonal)
    applied = (
        part_diag * centre
        - part_x * padded[:, :-2]
        - part_next * padded[:, 2:]
        - part_y * below_of(centre, 2)
        - above_of(part_y, 2) * above_of(centre, 2)
        - part_z * below_of(centre, 3)
        - above_of(part_z, 3) * above_of(centre, 3)
    )
    return centre + RELAX * (rhs_part - applied) / part_diag


def shards(source, trans_x, trans_y, trans_z, mortar_bot, mortar_top):
    local_x = source.shape[1]
    rows_y = source.shape[2]
    cells_z = source.shape[3]
    mortars = mortar_bot.shape[3]
    sub_count = lax.axis_size("sub")
    block_count = lax.axis_size("block")
    sub_index = lax.axis_index("sub")
    block_index = lax.axis_index("block")
    share = mortars // sub_count
    depth = 1
    global_x = lax.broadcasted_iota(jnp.int32, source.shape, 1) + sub_index * local_x
    masked_x = jnp.where(global_x > 0, trans_x, 0.0)
    upper_layer = from_behind(masked_x[:, 0:1], "sub", -1)
    coupling_x = widen_one(masked_x)
    coupling_next = widen_one(jnp.concatenate([masked_x[:, 1:], upper_layer], axis=1))
    raw_y = widen_one(trans_y)
    raw_z = widen_one(trans_z)
    wide_shape = coupling_x.shape
    wide_x = lax.broadcasted_iota(jnp.int32, wide_shape, 1) - depth + sub_index * local_x
    index_y = lax.broadcasted_iota(jnp.int32, wide_shape, 2)
    index_z = lax.broadcasted_iota(jnp.int32, wide_shape, 3)
    coupling_y = jnp.where(index_y > 0, raw_y, 0.0)
    coupling_z = jnp.where(index_z > 0, raw_z, 0.0)
    dirichlet_bot = jnp.where((index_z == 0) & (block_index > 0), raw_z, 0.0)
    dirichlet_top = jnp.where(
        (index_z == cells_z - 1) & (block_index < block_count - 1), raw_z, 0.0
    )
    diagonal = (
        coupling_x
        + coupling_next
        + coupling_y
        + above_of(coupling_y, 2)
        + coupling_z
        + above_of(coupling_z, 3)
        + dirichlet_bot
        + dirichlet_top
    )
    inside = (wide_x >= 0) & (wide_x < local_x * sub_count)
    diagonal = jnp.where(inside, diagonal, 1.0)
    coeffs = (coupling_x, coupling_next, coupling_y, coupling_z, diagonal)
    local_bot = dirichlet_bot[:, depth : depth + local_x]
    local_top = dirichlet_top[:, depth : depth + local_x]
    face_bot = mortar_bot.reshape(local_x * rows_y, mortars)
    face_top = mortar_top.reshape(local_x * rows_y, mortars)
    pressure = jnp.zeros_like(source)
    mortar_pair = jnp.zeros((2, mortars), jnp.float32)
    final_row = jnp.zeros((share,), jnp.float32)
    for outer_round in range(OUTER):
        bottom_data = jnp.dot(face_bot, mortar_pair[0], precision=HIGHEST).reshape(
            1, local_x, rows_y
        )
        top_data = jnp.dot(face_top, mortar_pair[1], precision=HIGHEST).reshape(1, local_x, rows_y)
        rhs = source + local_bot * bottom_data[..., None] + local_top * top_data[..., None]
        for pass_round in range(PASSES):
            padded = with_halo(pressure, (("sub", 1),), 1)
            pressure = relax_pass(padded, rhs, 1, coeffs)
        flux_bot = local_bot[..., 0] * (pressure[..., 0] - bottom_data)
        flux_top = local_top[..., cells_z - 1] * (pressure[..., cells_z - 1] - top_data)
        terms = jnp.stack(
            [
                jnp.dot(flux_bot.reshape(-1), face_bot, precision=HIGHEST),
                jnp.dot(flux_top.reshape(-1), face_top, precision=HIGHEST),
            ]
        )
        shares = lax.psum(terms, "sub")
        current_pair = mortar_pair
        nearby = with_halo(shares[None], (("block", 0),), 1)
        jumps = jnp.stack([nearby[0, 1] + nearby[1, 0], nearby[1, 1] + nearby[2, 0]])
        updated = current_pair + MORTAR_STEP * jumps
        mortar_pair = updated
        final_row = lax.dynamic_slice_in_dim(updated[1], sub_index * share, share, 0)
    return (pressure, final_row[None])


def solution(mesh):
    return jax.shard_map(
        shards,
        mesh=mesh,
        in_specs=(
            P("block", "sub", None, None),
            P("block", "sub", None, None),
            P("block", "sub", None, None),
            P("block", "sub", None, None),
            P("block", "sub", None, None),
            P("block", "sub", None, None),
        ),
        out_specs=(P("block", "sub", None, None), P("block", "sub")),
        check_vma=False,
    )
```

profile of v0, /device:TPU:12, one launch (start us, length us, event | category | flops | bytes accessed | tf_op | source)
XLA Modules:
  0.0 99.8 jit_solution(6974258271982418281)
XLA Ops:
  0.7 2.5 %collective-permute-start.2 = (f32[1,1,128,128]{2,1,3,0:T(1,128)S(1)}, f32[1,1,128,128]{2,1,3,0:T(1,128)S(1)}, u32[]{:S(2)}, u32[]{:S(2)}) collective-permute-start(f32[1,1,128,128]{2,1,3,0:T(1,128)S(1)} %broadcast.138), channel_id=1, source_target_pairs={{1,0},{2,1},{3,2},{5,4},{6,5},{7,6},{9,8},{10,9},{11,10},{13,12},{... | collective-permute-start | bytes 196616 | tf_op jit(solution)/shard_map/ppermute | solution.py:29
  3.2 3.5 %collective-permute-start.1 = (f32[1,1,128,128]{2,1,3,0:T(1,128)S(1)}, f32[1,1,128,128]{2,1,3,0:T(1,128)S(1)}, u32[]{:S(2)}, u32[]{:S(2)}) collective-permute-start(f32[1,1,128,128]{2,1,3,0:T(1,128)S(1)} %broadcast.138), channel_id=1, source_target_pairs={{0,1},{1,2},{2,3},{4,5},{5,6},{6,7},{8,9},{9,10},{10,11},{12,13},{... | collective-permute-start | bytes 196616 | tf_op jit(solution)/shard_map/ppermute | solution.py:28
  8.0 2.4 %collective-permute-start = (f32[1,1,128,128]{2,1,3,0:T(1,128)S(1)}, f32[1,1,128,128]{2,1,3,0:T(1,128)S(1)}, u32[]{:S(2)}, u32[]{:S(2)}) collective-permute-start(f32[1,1,128,128]{2,1,3,0:T(1,128)S(1)} %slice.352), channel_id=1, source_target_pairs={{1,0},{2,1},{3,2},{5,4},{6,5},{7,6},{9,8},{10,9},{11,10},{13,12},{... | collective-permute-start | bytes 196616 | tf_op jit(solution)/shard_map/ppermute | solution.py:18
  16.7 3.5 %collective-permute-start.3 = (f32[1,1,128,128]{2,1,3,0:T(1,128)S(1)}, f32[1,1,128,128]{2,1,3,0:T(1,128)S(1)}, u32[]{:S(2)}, u32[]{:S(2)}) collective-permute-start(f32[1,1,128,128]{2,1,3,0:T(1,128)S(1)} %get-tuple-element.23), channel_id=1, source_target_pairs={{0,1},{1,2},{2,3},{4,5},{5,6},{6,7},{8,9},{9,10},{10,11},{12,13},{... | collective-permute-start | bytes 196616 | tf_op jit(solution)/shard_map/ppermute | solution.py:28
  20.2 2.4 %collective-permute-start.4 = (f32[1,1,128,128]{2,1,3,0:T(1,128)S(1)}, f32[1,1,128,128]{2,1,3,0:T(1,128)S(1)}, u32[]{:S(2)}, u32[]{:S(2)}) collective-permute-start(f32[1,1,128,128]{2,1,3,0:T(1,128)S(1)} %get-tuple-element.24), channel_id=1, source_target_pairs={{1,0},{2,1},{3,2},{5,4},{6,5},{7,6},{9,8},{10,9},{11,10},{13,12},{... | collective-permute-start | bytes 196616 | tf_op jit(solution)/shard_map/ppermute | solution.py:29
  22.9 3.5 %collective-permute-done.4 = f32[1,1,128,128]{2,1,3,0:T(1,128)S(1)} collective-permute-done((f32[1,1,128,128]{2,1,3,0:T(1,128)S(1)}, f32[1,1,128,128]{2,1,3,0:T(1,128)S(1)}, u32[]{:S(2)}, u32[]{:S(2)}) %collective-permute-start.4) | collective-permute-done | bytes 65568 | tf_op jit(solution)/shard_map/ppermute | solution.py:29
  27.3 3.5 %collective-permute-start.5 = (f32[1,1,128,128]{2,1,3,0:T(1,128)S(1)}, f32[1,1,128,128]{2,1,3,0:T(1,128)S(1)}, u32[]{:S(2)}, u32[]{:S(2)}) collective-permute-start(f32[1,1,128,128]{2,1,3,0:T(1,128)S(1)} %get-tuple-element.21), channel_id=1, source_target_pairs={{0,1},{1,2},{2,3},{4,5},{5,6},{6,7},{8,9},{9,10},{10,11},{12,13},{... | collective-permute-start | bytes 196616 | tf_op jit(solution)/shard_map/ppermute | solution.py:28
  30.8 2.4 %collective-permute-start.6 = (f32[1,1,128,128]{2,1,3,0:T(1,128)S(1)}, f32[1,1,128,128]{2,1,3,0:T(1,128)S(1)}, u32[]{:S(2)}, u32[]{:S(2)}) collective-permute-start(f32[1,1,128,128]{2,1,3,0:T(1,128)S(1)} %get-tuple-element.22), channel_id=1, source_target_pairs={{1,0},{2,1},{3,2},{5,4},{6,5},{7,6},{9,8},{10,9},{11,10},{13,12},{... | collective-permute-start | bytes 196616 | tf_op jit(solution)/shard_map/ppermute | solution.py:29
  33.5 3.5 %collective-permute-done.6 = f32[1,1,128,128]{2,1,3,0:T(1,128)S(1)} collective-permute-done((f32[1,1,128,128]{2,1,3,0:T(1,128)S(1)}, f32[1,1,128,128]{2,1,3,0:T(1,128)S(1)}, u32[]{:S(2)}, u32[]{:S(2)}) %collective-permute-start.6) | collective-permute-done | bytes 65568 | tf_op jit(solution)/shard_map/ppermute | solution.py:29
  38.5 8.8 %psum.14 = f32[1,2,256]{2,1,0:T(2,128)S(1)} all-reduce(f32[1,2,256]{2,1,0:T(2,128)S(1)} %maximum_bitcast_fusion), channel_id=1, replica_groups=mesh['block'=8,'sub'=4] {'sub'}, use_global_device_ids=true, to_apply=%region_0.1 | all-reduce | flops 512 | bytes 4096 | tf_op jit(solution)/shard_map/psum | solution.py:140
  47.3 1.9 %collective-permute-start.8 = (f32[1,2,256]{2,1,0:T(2,128)S(1)}, f32[1,2,256]{2,1,0:T(2,128)S(1)}, u32[]{:S(2)}, u32[]{:S(2)}) collective-permute-start(f32[1,2,256]{2,1,0:T(2,128)S(1)} %psum.14), channel_id=1, source_target_pairs={{4,0},{8,4},{12,8},{16,12},{20,16},{24,20},{28,24},{5,1},{9,5},{13... | collective-permute-start | bytes 6152 | tf_op jit(solution)/shard_map/ppermute | solution.py:29
  49.2 2.4 %collective-permute-start.7 = (f32[1,2,256]{2,1,0:T(2,128)S(1)}, f32[1,2,256]{2,1,0:T(2,128)S(1)}, u32[]{:S(2)}, u32[]{:S(2)}) collective-permute-start(f32[1,2,256]{2,1,0:T(2,128)S(1)} %psum.14), channel_id=1, source_target_pairs={{0,4},{4,8},{8,12},{12,16},{16,20},{20,24},{24,28},{1,5},{5,9},{9,... | collective-permute-start | bytes 6152 | tf_op jit(solution)/shard_map/ppermute | solution.py:28
  51.7 1.9 %collective-permute-start.9 = (f32[1,1,128,128]{2,1,3,0:T(1,128)S(1)}, f32[1,1,128,128]{2,1,3,0:T(1,128)S(1)}, u32[]{:S(2)}, u32[]{:S(2)}) collective-permute-start(f32[1,1,128,128]{2,1,3,0:T(1,128)S(1)} %get-tuple-element.19), channel_id=1, source_target_pairs={{0,1},{1,2},{2,3},{4,5},{5,6},{6,7},{8,9},{9,10},{10,11},{12,13},{... | collective-permute-start | bytes 196616 | tf_op jit(solution)/shard_map/ppermute | solution.py:28
  53.6 3.9 %collective-permute-start.10 = (f32[1,1,128,128]{2,1,3,0:T(1,128)S(1)}, f32[1,1,128,128]{2,1,3,0:T(1,128)S(1)}, u32[]{:S(2)}, u32[]{:S(2)}) collective-permute-start(f32[1,1,128,128]{2,1,3,0:T(1,128)S(1)} %get-tuple-element.20), channel_id=1, source_target_pairs={{1,0},{2,1},{3,2},{5,4},{6,5},{7,6},{9,8},{10,9},{11,10},{13,12},{... | collective-permute-start | bytes 196616 | tf_op jit(solution)/shard_map/ppermute | solution.py:29
  61.4 3.1 %collective-permute-start.11 = (f32[1,1,128,128]{2,1,3,0:T(1,128)S(1)}, f32[1,1,128,128]{2,1,3,0:T(1,128)S(1)}, u32[]{:S(2)}, u32[]{:S(2)}) collective-permute-start(f32[1,1,128,128]{2,1,3,0:T(1,128)S(1)} %get-tuple-element.15), channel_id=1, source_target_pairs={{0,1},{1,2},{2,3},{4,5},{5,6},{6,7},{8,9},{9,10},{10,11},{12,13},{... | collective-permute-start | bytes 196616 | tf_op jit(solution)/shard_map/ppermute | solution.py:28
  64.5 2.8 %collective-permute-start.12 = (f32[1,1,128,128]{2,1,3,0:T(1,128)S(1)}, f32[1,1,128,128]{2,1,3,0:T(1,128)S(1)}, u32[]{:S(2)}, u32[]{:S(2)}) collective-permute-start(f32[1,1,128,128]{2,1,3,0:T(1,128)S(1)} %get-tuple-element.16), channel_id=1, source_target_pairs={{1,0},{2,1},{3,2},{5,4},{6,5},{7,6},{9,8},{10,9},{11,10},{13,12},{... | collective-permute-start | bytes 196616 | tf_op jit(solution)/shard_map/ppermute | solution.py:29
  67.6 3.1 %collective-permute-done.12 = f32[1,1,128,128]{2,1,3,0:T(1,128)S(1)} collective-permute-done((f32[1,1,128,128]{2,1,3,0:T(1,128)S(1)}, f32[1,1,128,128]{2,1,3,0:T(1,128)S(1)}, u32[]{:S(2)}, u32[]{:S(2)}) %collective-permute-start.12) | collective-permute-done | bytes 65568 | tf_op jit(solution)/shard_map/ppermute | solution.py:29
  71.6 1.9 %collective-permute-start.13 = (f32[1,1,128,128]{2,1,3,0:T(1,128)S(1)}, f32[1,1,128,128]{2,1,3,0:T(1,128)S(1)}, u32[]{:S(2)}, u32[]{:S(2)}) collective-permute-start(f32[1,1,128,128]{2,1,3,0:T(1,128)S(1)} %get-tuple-element.13), channel_id=1, source_target_pairs={{0,1},{1,2},{2,3},{4,5},{5,6},{6,7},{8,9},{9,10},{10,11},{12,13},{... | collective-permute-start | bytes 196616 | tf_op jit(solution)/shard_map/ppermute | solution.py:28
  73.5 3.9 %collective-permute-start.14 = (f32[1,1,128,128]{2,1,3,0:T(1,128)S(1)}, f32[1,1,128,128]{2,1,3,0:T(1,128)S(1)}, u32[]{:S(2)}, u32[]{:S(2)}) collective-permute-start(f32[1,1,128,128]{2,1,3,0:T(1,128)S(1)} %get-tuple-element.14), channel_id=1, source_target_pairs={{1,0},{2,1},{3,2},{5,4},{6,5},{7,6},{9,8},{10,9},{11,10},{13,12},{... | collective-permute-start | bytes 196616 | tf_op jit(solution)/shard_map/ppermute | solution.py:29
  77.7 1.9 %collective-permute-done.14 = f32[1,1,128,128]{2,1,3,0:T(1,128)S(1)} collective-permute-done((f32[1,1,128,128]{2,1,3,0:T(1,128)S(1)}, f32[1,1,128,128]{2,1,3,0:T(1,128)S(1)}, u32[]{:S(2)}, u32[]{:S(2)}) %collective-permute-start.14) | collective-permute-done | bytes 65568 | tf_op jit(solution)/shard_map/ppermute | solution.py:29
  81.1 10.3 %psum.15 = f32[1,2,256]{2,1,0:T(2,128)S(1)} all-reduce(f32[1,2,256]{2,1,0:T(2,128)S(1)} %maximum_bitcast_fusion.1), channel_id=1, replica_groups=mesh['block'=8,'sub'=4] {'sub'}, use_global_device_ids=true, to_apply=%region_1.2 | all-reduce | flops 512 | bytes 4096 | tf_op jit(solution)/shard_map/psum | solution.py:140
  91.5 1.9 %collective-permute-start.16 = (f32[1,2,256]{2,1,0:T(2,128)S(1)}, f32[1,2,256]{2,1,0:T(2,128)S(1)}, u32[]{:S(2)}, u32[]{:S(2)}) collective-permute-start(f32[1,2,256]{2,1,0:T(2,128)S(1)} %psum.15), channel_id=1, source_target_pairs={{4,0},{8,4},{12,8},{16,12},{20,16},{24,20},{28,24},{5,1},{9,5},{13... | collective-permute-start | bytes 6152 | tf_op jit(solution)/shard_map/ppermute | solution.py:29
  93.4 2.4 %collective-permute-start.15 = (f32[1,2,256]{2,1,0:T(2,128)S(1)}, f32[1,2,256]{2,1,0:T(2,128)S(1)}, u32[]{:S(2)}, u32[]{:S(2)}) collective-permute-start(f32[1,2,256]{2,1,0:T(2,128)S(1)} %psum.15), channel_id=1, source_target_pairs={{0,4},{4,8},{8,12},{12,16},{16,20},{20,24},{24,28},{1,5},{5,9},{9,... | collective-permute-start | bytes 6152 | tf_op jit(solution)/shard_map/ppermute | solution.py:28
  96.7 2.5 %collective-permute-done.15 = f32[1,2,256]{2,1,0:T(2,128)S(1)} collective-permute-done((f32[1,2,256]{2,1,0:T(2,128)S(1)}, f32[1,2,256]{2,1,0:T(2,128)S(1)}, u32[]{:S(2)}, u32[]{:S(2)}) %collective-permute-start.15) | collective-permute-done | bytes 2080 | tf_op jit(solution)/shard_map/ppermute | solution.py:28
  (79 shorter events, 18.9 us)
Async XLA Ops:
  0.6 10.5 %copy-start = (f32[1,4,128,256]{3,2,1,0:T(8,128)S(1)}, f32[1,4,128,256]{3,2,1,0:T(8,128)}, u32[]{:S(2)}) copy-start(f32[1,4,128,256]{3,2,1,0:T(8,128)} %param.10) | copy-start | bytes 1572868
  0.7 14.8 %collective-permute-start.2 = (f32[1,1,128,128]{2,1,3,0:T(1,128)S(1)}, f32[1,1,128,128]{2,1,3,0:T(1,128)S(1)}, u32[]{:S(2)}, u32[]{:S(2)}) collective-permute-start(f32[1,1,128,128]{2,1,3,0:T(1,128)S(1)} %broadcast.138), channel_id=1, source_target_pairs={{1,0},{2,1},{3,2},{5,4},{6,5},{7,6},{9,8},{10,9},{11,10},{13,12},{... | collective-permute-start | bytes 196616 | tf_op jit(solution)/shard_map/ppermute | solution.py:29
  3.2 12.4 %collective-permute-start.1 = (f32[1,1,128,128]{2,1,3,0:T(1,128)S(1)}, f32[1,1,128,128]{2,1,3,0:T(1,128)S(1)}, u32[]{:S(2)}, u32[]{:S(2)}) collective-permute-start(f32[1,1,128,128]{2,1,3,0:T(1,128)S(1)} %broadcast.138), channel_id=1, source_target_pairs={{0,1},{1,2},{2,3},{4,5},{5,6},{6,7},{8,9},{9,10},{10,11},{12,13},{... | collective-permute-start | bytes 196616 | tf_op jit(solution)/shard_map/ppermute | solution.py:28
  7.8 2.7 %copy-start.1 = (f32[1,4,128,256]{3,2,1,0:T(8,128)S(1)}, f32[1,4,128,256]{3,2,1,0:T(8,128)}, u32[]{:S(2)}) copy-start(f32[1,4,128,256]{3,2,1,0:T(8,128)} %param.11) | copy-start | bytes 1572868
  8.0 6.2 %collective-permute-start = (f32[1,1,128,128]{2,1,3,0:T(1,128)S(1)}, f32[1,1,128,128]{2,1,3,0:T(1,128)S(1)}, u32[]{:S(2)}, u32[]{:S(2)}) collective-permute-start(f32[1,1,128,128]{2,1,3,0:T(1,128)S(1)} %slice.352), channel_id=1, source_target_pairs={{1,0},{2,1},{3,2},{5,4},{6,5},{7,6},{9,8},{10,9},{11,10},{13,12},{... | collective-permute-start | bytes 196616 | tf_op jit(solution)/shard_map/ppermute | solution.py:18
  11.1 1.0 copy-start.6
  15.1 22.7 %copy-start.2 = (f32[1,6,128,128]{2,1,3,0:T(8,128)}, f32[1,6,128,128]{2,1,3,0:T(8,128)S(1)}, u32[]{:S(2)}) copy-start(f32[1,6,128,128]{2,1,3,0:T(8,128)S(1)} %get-tuple-element.25) | copy-start | bytes 1179652
  15.1 22.7 %copy-start.4 = (f32[1,6,128,128]{2,1,3,0:T(8,128)}, f32[1,6,128,128]{2,1,3,0:T(8,128)S(1)}, u32[]{:S(2)}) copy-start(f32[1,6,128,128]{2,1,3,0:T(8,128)S(1)} %get-tuple-element.26) | copy-start | bytes 1179652
  16.7 6.2 %collective-permute-start.3 = (f32[1,1,128,128]{2,1,3,0:T(1,128)S(1)}, f32[1,1,128,128]{2,1,3,0:T(1,128)S(1)}, u32[]{:S(2)}, u32[]{:S(2)}) collective-permute-start(f32[1,1,128,128]{2,1,3,0:T(1,128)S(1)} %get-tuple-element.23), channel_id=1, source_target_pairs={{0,1},{1,2},{2,3},{4,5},{5,6},{6,7},{8,9},{9,10},{10,11},{12,13},{... | collective-permute-start | bytes 196616 | tf_op jit(solution)/shard_map/ppermute | solution.py:28
  20.2 6.2 %collective-permute-start.4 = (f32[1,1,128,128]{2,1,3,0:T(1,128)S(1)}, f32[1,1,128,128]{2,1,3,0:T(1,128)S(1)}, u32[]{:S(2)}, u32[]{:S(2)}) collective-permute-start(f32[1,1,128,128]{2,1,3,0:T(1,128)S(1)} %get-tuple-element.24), channel_id=1, source_target_pairs={{1,0},{2,1},{3,2},{5,4},{6,5},{7,6},{9,8},{10,9},{11,10},{13,12},{... | collective-permute-start | bytes 196616 | tf_op jit(solution)/shard_map/ppermute | solution.py:29
  27.3 6.2 %collective-permute-start.5 = (f32[1,1,128,128]{2,1,3,0:T(1,128)S(1)}, f32[1,1,128,128]{2,1,3,0:T(1,128)S(1)}, u32[]{:S(2)}, u32[]{:S(2)}) collective-permute-start(f32[1,1,128,128]{2,1,3,0:T(1,128)S(1)} %get-tuple-element.21), channel_id=1, source_target_pairs={{0,1},{1,2},{2,3},{4,5},{5,6},{6,7},{8,9},{9,10},{10,11},{12,13},{... | collective-permute-start | bytes 196616 | tf_op jit(solution)/shard_map/ppermute | solution.py:28
  30.8 6.2 %collective-permute-start.6 = (f32[1,1,128,128]{2,1,3,0:T(1,128)S(1)}, f32[1,1,128,128]{2,1,3,0:T(1,128)S(1)}, u32[]{:S(2)}, u32[]{:S(2)}) collective-permute-start(f32[1,1,128,128]{2,1,3,0:T(1,128)S(1)} %get-tuple-element.22), channel_id=1, source_target_pairs={{1,0},{2,1},{3,2},{5,4},{6,5},{7,6},{9,8},{10,9},{11,10},{13,12},{... | collective-permute-start | bytes 196616 | tf_op jit(solution)/shard_map/ppermute | solution.py:29
  47.3 10.3 %collective-permute-start.8 = (f32[1,2,256]{2,1,0:T(2,128)S(1)}, f32[1,2,256]{2,1,0:T(2,128)S(1)}, u32[]{:S(2)}, u32[]{:S(2)}) collective-permute-start(f32[1,2,256]{2,1,0:T(2,128)S(1)} %psum.14), channel_id=1, source_target_pairs={{4,0},{8,4},{12,8},{16,12},{20,16},{24,20},{28,24},{5,1},{9,5},{13... | collective-permute-start | bytes 6152 | tf_op jit(solution)/shard_map/ppermute | solution.py:29
  49.2 8.4 %collective-permute-start.7 = (f32[1,2,256]{2,1,0:T(2,128)S(1)}, f32[1,2,256]{2,1,0:T(2,128)S(1)}, u32[]{:S(2)}, u32[]{:S(2)}) collective-permute-start(f32[1,2,256]{2,1,0:T(2,128)S(1)} %psum.14), channel_id=1, source_target_pairs={{0,4},{4,8},{8,12},{12,16},{16,20},{20,24},{24,28},{1,5},{5,9},{9,... | collective-permute-start | bytes 6152 | tf_op jit(solution)/shard_map/ppermute | solution.py:28
  51.7 7.0 %collective-permute-start.9 = (f32[1,1,128,128]{2,1,3,0:T(1,128)S(1)}, f32[1,1,128,128]{2,1,3,0:T(1,128)S(1)}, u32[]{:S(2)}, u32[]{:S(2)}) collective-permute-start(f32[1,1,128,128]{2,1,3,0:T(1,128)S(1)} %get-tuple-element.19), channel_id=1, source_target_pairs={{0,1},{1,2},{2,3},{4,5},{5,6},{6,7},{8,9},{9,10},{10,11},{12,13},{... | collective-permute-start | bytes 196616 | tf_op jit(solution)/shard_map/ppermute | solution.py:28
  53.6 6.7 %collective-permute-start.10 = (f32[1,1,128,128]{2,1,3,0:T(1,128)S(1)}, f32[1,1,128,128]{2,1,3,0:T(1,128)S(1)}, u32[]{:S(2)}, u32[]{:S(2)}) collective-permute-start(f32[1,1,128,128]{2,1,3,0:T(1,128)S(1)} %get-tuple-element.20), channel_id=1, source_target_pairs={{1,0},{2,1},{3,2},{5,4},{6,5},{7,6},{9,8},{10,9},{11,10},{13,12},{... | collective-permute-start | bytes 196616 | tf_op jit(solution)/shard_map/ppermute | solution.py:29
  57.6 2.7 %copy-start.3 = (f32[1,6,128,128]{2,1,3,0:T(8,128)S(1)}, f32[1,6,128,128]{2,1,3,0:T(8,128)}, u32[]{:S(2)}) copy-start(f32[1,6,128,128]{2,1,3,0:T(8,128)} %copy-done.2) | copy-start | bytes 1179652
  57.6 2.7 %copy-start.5 = (f32[1,6,128,128]{2,1,3,0:T(8,128)S(1)}, f32[1,6,128,128]{2,1,3,0:T(8,128)}, u32[]{:S(2)}) copy-start(f32[1,6,128,128]{2,1,3,0:T(8,128)} %copy-done.4) | copy-start | bytes 1179652
  61.4 6.2 %collective-permute-start.11 = (f32[1,1,128,128]{2,1,3,0:T(1,128)S(1)}, f32[1,1,128,128]{2,1,3,0:T(1,128)S(1)}, u32[]{:S(2)}, u32[]{:S(2)}) collective-permute-start(f32[1,1,128,128]{2,1,3,0:T(1,128)S(1)} %get-tuple-element.15), channel_id=1, source_target_pairs={{0,1},{1,2},{2,3},{4,5},{5,6},{6,7},{8,9},{9,10},{10,11},{12,13},{... | collective-permute-start | bytes 196616 | tf_op jit(solution)/shard_map/ppermute | solution.py:28
  64.5 6.2 %collective-permute-start.12 = (f32[1,1,128,128]{2,1,3,0:T(1,128)S(1)}, f32[1,1,128,128]{2,1,3,0:T(1,128)S(1)}, u32[]{:S(2)}, u32[]{:S(2)}) collective-permute-start(f32[1,1,128,128]{2,1,3,0:T(1,128)S(1)} %get-tuple-element.16), channel_id=1, source_target_pairs={{1,0},{2,1},{3,2},{5,4},{6,5},{7,6},{9,8},{10,9},{11,10},{13,12},{... | collective-permute-start | bytes 196616 | tf_op jit(solution)/shard_map/ppermute | solution.py:29
  71.6 6.2 %collective-permute-start.13 = (f32[1,1,128,128]{2,1,3,0:T(1,128)S(1)}, f32[1,1,128,128]{2,1,3,0:T(1,128)S(1)}, u32[]{:S(2)}, u32[]{:S(2)}) collective-permute-start(f32[1,1,128,128]{2,1,3,0:T(1,128)S(1)} %get-tuple-element.13), channel_id=1, source_target_pairs={{0,1},{1,2},{2,3},{4,5},{5,6},{6,7},{8,9},{9,10},{10,11},{12,13},{... | collective-permute-start | bytes 196616 | tf_op jit(solution)/shard_map/ppermute | solution.py:28
  73.5 6.2 %collective-permute-start.14 = (f32[1,1,128,128]{2,1,3,0:T(1,128)S(1)}, f32[1,1,128,128]{2,1,3,0:T(1,128)S(1)}, u32[]{:S(2)}, u32[]{:S(2)}) collective-permute-start(f32[1,1,128,128]{2,1,3,0:T(1,128)S(1)} %get-tuple-element.14), channel_id=1, source_target_pairs={{1,0},{2,1},{3,2},{5,4},{6,5},{7,6},{9,8},{10,9},{11,10},{13,12},{... | collective-permute-start | bytes 196616 | tf_op jit(solution)/shard_map/ppermute | solution.py:29
  91.5 5.2 %collective-permute-start.16 = (f32[1,2,256]{2,1,0:T(2,128)S(1)}, f32[1,2,256]{2,1,0:T(2,128)S(1)}, u32[]{:S(2)}, u32[]{:S(2)}) collective-permute-start(f32[1,2,256]{2,1,0:T(2,128)S(1)} %psum.15), channel_id=1, source_target_pairs={{4,0},{8,4},{12,8},{16,12},{20,16},{24,20},{28,24},{5,1},{9,5},{13... | collective-permute-start | bytes 6152 | tf_op jit(solution)/shard_map/ppermute | solution.py:29
  93.4 5.8 %collective-permute-start.15 = (f32[1,2,256]{2,1,0:T(2,128)S(1)}, f32[1,2,256]{2,1,0:T(2,128)S(1)}, u32[]{:S(2)}, u32[]{:S(2)}) collective-permute-start(f32[1,2,256]{2,1,0:T(2,128)S(1)} %psum.15), channel_id=1, source_target_pairs={{0,4},{4,8},{8,12},{12,16},{16,20},{20,24},{24,28},{1,5},{5,9},{9,... | collective-permute-start | bytes 6152 | tf_op jit(solution)/shard_map/ppermute | solution.py:28
  (2 other events, 1.9 us)
where the time goes:
time: 100 us; the launch traced here: 99.8 us
  starting transfers between devices  46.2 us (46%)
  blocking collectives  19.1 us (19%)
  waiting for transfers between devices  17.4 us (17%)
  other arithmetic  7.05 us (7%)
  local copies, waits for them, and re-layouts  5.58 us (6%)
  matrix products  3.32 us (3%)
  between operations  1.12 us (1%)
    ppermute x8, starting transfers between devices, with_halo(): before = lax.ppermute(last, axis, up)  22.2 us
    ppermute x8, starting transfers between devices, with_halo(): after = lax.ppermute(leading, axis, down)  21.7 us
    psum x2, blocking collectives, shards(): shares = lax.psum(terms, 'sub')  19.1 us
    ppermute x8, waiting for transfers between devices, with_halo(): after = lax.ppermute(leading, axis, down)  13.7 us
    unnamed x23, local copies, waits for them, and re-layouts  4.42 us
    add x5, other arithmetic, relax_pass(): return centre + RELAX * (rhs_part - applied) / part_diag  4.21 us
    ppermute x8, waiting for transfers between devices, with_halo(): before = lax.ppermute(last, axis, up)  3.74 us
    ppermute x1, starting transfers between devices, from_behind(): return lax.ppermute(block, axis, route)  2.36 us
  transfers between devices with their start and end apart: 17, of which 10 were waited for; matrix products, arithmetic and copies ran while one was open for 6% of the time, Pallas kernels for 0%

commit v1 on v0

v1 whole, which is shorter than its diff:
```python
import jax
import jax.numpy as jnp
from jax import lax
from jax.experimental import pallas as pl
from jax.experimental.pallas import tpu as pltpu
from jax.sharding import PartitionSpec as P

RELAX = 0.8
KEEP = 1.0 - RELAX
MORTAR_STEP = 0.05
F32 = jnp.float32
EDGE = 5
REST = 8
HALO = 2
VMEM = pl.BlockSpec(memory_space=pltpu.VMEM)


def prev(v, axis):
    return pltpu.roll(v, 1, axis)


def following(v, axis):
    return pltpu.roll(v, v.shape[axis] - 1, axis)


class Layer:
    def __init__(self, trans_y, trans_z, has_bot, has_top):
        rows = lax.broadcasted_iota(jnp.int32, trans_y.shape, 0)
        cols = lax.broadcasted_iota(jnp.int32, trans_y.shape, 1)
        self.first = cols == 0
        self.last = cols == trans_y.shape[1] - 1
        self.cy = jnp.where(rows > 0, trans_y, 0.0)
        self.cz = jnp.where(self.first, 0.0, trans_z)
        self.dbot = jnp.where(self.first, trans_z, 0.0) * has_bot
        self.dtop = jnp.where(self.last, trans_z, 0.0) * has_top
        self.diag = (
            self.cy
            + following(self.cy, 0)
            + self.cz
            + following(self.cz, 1)
            + self.dbot
            + self.dtop
        )

    def around(self, p):
        return (
            self.cy * prev(p, 0)
            + following(self.cy * p, 0)
            + self.cz * prev(p, 1)
            + following(self.cz * p, 1)
        )


def flags():
    block = lax.axis_index("block")
    sub = lax.axis_index("sub")
    has_bot = (block > 0).astype(F32)
    has_top = (block < lax.axis_size("block") - 1).astype(F32)
    has_below = (sub > 0).astype(F32)
    has_above = (sub < lax.axis_size("sub") - 1).astype(F32)
    return has_bot, has_top, has_below, has_above


def by_parity(axis, first, second, upward, downward):
    even = lax.rem(lax.axis_index(axis), 2) == 0

    @pl.when(even)
    def _():
        upward(first)
        downward(second)

    @pl.when(jnp.logical_not(even))
    def _():
        upward(second)
        downward(first)


def edge_kernel(src, tx, ty, tz, out_a, out_b):
    count = src.shape[1]
    has_bot, has_top, has_below, _ = flags()

    def layer(x):
        return Layer(ty[0, x], tz[0, x], has_bot, has_top)

    low = layer(0)
    w_low = RELAX / (low.diag + tx[0, 0] * has_below + tx[0, 1])
    p_low = w_low * src[0, 0]
    p_next = RELAX * src[0, 1] / (layer(1).diag + tx[0, 1] + tx[0, 2])
    q_low = KEEP * p_low + w_low * (src[0, 0] + tx[0, 1] * p_next + low.around(p_low))
    top = count - 1
    p_top = RELAX * src[0, top - 1] / (layer(top - 1).diag + tx[0, top - 1] + tx[0, top])

    def upward(ref):
        ref[0] = src[0, top]
        ref[1] = tx[0, top]
        ref[2] = ty[0, top]
        ref[3] = tz[0, top]
        ref[4] = p_top

    def downward(ref):
        ref[0] = tx[0, 0]
        ref[1] = p_low
        ref[2] = q_low
        ref[3] = w_low
        ref[4] = src[0, 0]

    by_parity("sub", out_a, out_b, upward, downward)


def rest_kernel(src, tx, ty, tz, bot, top, out_a, out_b, rows_a, rows_b):
    count = src.shape[1]

    def upward(ref):
        for i, part in enumerate((src, tx, ty, tz)):
            ref[i] = part[0, count - 2]
            ref[i + 4] = part[0, count - 2]

    def downward(ref):
        for i, part in enumerate((ty, tz)):
            ref[i] = part[0, 0]
        for i, part in enumerate((src, tx, ty, tz)):
            ref[i + 2] = part[0, 1]
        ref[6] = tx[0, 2]
        ref[7] = tx[0, 2]

    by_parity("sub", out_a, out_b, upward, downward)

    def rows_up(ref):
        ref[0:HALO] = bot[0, count - HALO : count]
        ref[HALO : 2 * HALO] = top[0, count - HALO : count]

    def rows_down(ref):
        ref[0:HALO] = bot[0, 0:HALO]
        ref[HALO : 2 * HALO] = top[0, 0:HALO]

    by_parity("sub", rows_a, rows_b, rows_up, rows_down)


def traces(flux, basis):
    return sum(
        jnp.sum(f * basis[0, x], axis=0, keepdims=True) for x, f in enumerate(flux)
    )


def place_shares(cbot, ctop, out_a, out_b):
    def upward(ref):
        ref[...] = ctop

    def downward(ref):
        ref[...] = cbot

    by_parity("block", out_a, out_b, upward, downward)


def first_kernel(src, tx, ty, tz, bot, top, got_a, got_b, p_out, halo_a, halo_b, sh_a, sh_b, above, below):
    count = src.shape[1]
    has_bot, has_top, has_below, has_above = flags()

    def take_above(ref):
        above[...] = ref[...]

    def take_below(ref):
        below[...] = ref[...]

    by_parity("sub", got_a, got_b, take_above, take_below)
    source = {x: src[0, x] for x in range(count)}
    source[-1] = below[0]
    cx = {x: tx[0, x] for x in range(1, count)}
    cx[-1] = below[1]
    cx[0] = tx[0, 0] * has_below
    cx[count] = above[0] * has_above
    layers = {x: Layer(ty[0, x], tz[0, x], has_bot, has_top) for x in range(count)}
    layers[-1] = Layer(below[2], below[3], has_bot, has_top)
    w = {x: RELAX / (layers[x].diag + cx[x] + cx[x + 1]) for x in range(-1, count)}
    p1 = {x: w[x] * source[x] for x in range(-1, count)}
    p1[-2] = below[4]
    p1[count] = above[1]

    def step(p, x):
        return KEEP * p[x] + w[x] * (
            source[x] + cx[x] * p[x - 1] + cx[x + 1] * p[x + 1] + layers[x].around(p[x])
        )

    p2 = {x: step(p1, x) for x in range(-1, count)}
    p2[count] = above[2] + above[3] * cx[count] * p1[count - 1]
    p3 = {x: step(p2, x) for x in range(count)}
    for x in range(count):
        p_out[x] = p3[x]
    width = halo_a.shape[0]

    def upward(ref):
        for i in range(width):
            ref[i] = p3[count - width + i]

    def downward(ref):
        for i in range(width):
            ref[i] = p3[i]

    by_parity("sub", halo_a, halo_b, upward, downward)
    end = src.shape[3] - 1
    flux_bot = [layers[x].dbot[:, 0:1] * p3[x][:, 0:1] for x in range(count)]
    flux_top = [layers[x].dtop[:, end:] * p3[x][:, end:] for x in range(count)]
    place_shares(traces(flux_bot, bot), traces(flux_top, top), sh_a, sh_b)


def second_kernel(
    src, tx, ty, tz, bot, top, got_a, got_b, rest_a, rest_b, rows_a, rows_b,
    p_in, halo_a, halo_b, *rest,
):
    parts = rest[:-12]
    p_out, cbot_out, ctop_out, mortar_out = rest[-12:-8]
    above, below, more_above, more_below, rows_above, rows_below, p_above, p_below = rest[-8:]
    count = src.shape[1]
    has_bot, has_top, has_below, has_above = flags()
    for pair, (up, down) in (
        ((got_a, got_b), (above, below)),
        ((rest_a, rest_b), (more_above, more_below)),
        ((rows_a, rows_b), (rows_above, rows_below)),
        ((halo_a, halo_b), (p_above, p_below)),
    ):
        def take_above(ref, to=up):
            to[...] = ref[...]

        def take_below(ref, to=down):
            to[...] = ref[...]

        by_parity("sub", *pair, take_above, take_below)

    jumps = MORTAR_STEP * sum(part[...] for part in parts)
    even = lax.rem(lax.axis_index("block"), 2) == 0
    own = jnp.where(even, jumps[0:1], jumps[1:2])
    under = jnp.where(even, jumps[1:2], jumps[0:1])
    mortar_out[...] = own

    source = {x: src[0, x] for x in range(count)}
    source[-1] = below[0]
    source[-2] = more_below[0]
    source[count] = above[4]
    source[count + 1] = more_above[2]
    cx = {x: tx[0, x] for x in range(1, count)}
    cx[-2] = more_below[1]
    cx[-1] = below[1]
    cx[0] = tx[0, 0] * has_below
    cx[count] = above[0] * has_above
    cx[count + 1] = more_above[3]
    cx[count + 2] = more_above[6]
    ty_of = {x: ty[0, x] for x in range(count)}
    tz_of = {x: tz[0, x] for x in range(count)}
    ty_of[-1], tz_of[-1] = below[2], below[3]
    ty_of[-2], tz_of[-2] = more_below[2], more_below[3]
    ty_of[count], tz_of[count] = more_above[0], more_above[1]
    ty_of[count + 1], tz_of[count + 1] = more_above[4], more_above[5]
    reach = range(-HALO, count + HALO)
    layers = {x: Layer(ty_of[x], tz_of[x], has_bot, has_top) for x in reach}
    w = {x: RELAX / (layers[x].diag + cx[x] + cx[x + 1]) for x in reach}

    def basis(ref, rows, face, x):
        if x < 0:
            return rows[1][face * HALO + x + HALO]
        if x >= count:
            return rows[0][face * HALO + x - count]
        return ref[0, x]

    halves = (rows_above, rows_below)
    gbot = {x: jnp.sum(basis(bot, halves, 0, x) * under, axis=1, keepdims=True) for x in reach}
    gtop = {x: jnp.sum(basis(top, halves, 1, x) * own, axis=1, keepdims=True) for x in reach}
    rhs = {
        x: source[x] + layers[x].dbot * gbot[x] + layers[x].dtop * gtop[x] for x in reach
    }
    width = p_above.shape[0]
    p = {x: p_in[x] for x in range(count)}
    for i in range(width):
        p[count + i] = p_above[i]
        p[i - width] = p_below[i]
    for margin in range(HALO, -1, -1):
        old = p
        p = {
            x: KEEP * old[x]
            + w[x] * (rhs[x] + cx[x] * old[x - 1] + cx[x + 1] * old[x + 1] + layers[x].around(old[x]))
            for x in range(-margin, count + margin)
        }
    for x in range(count):
        p_out[0, x] = p[x]
    end = src.shape[3] - 1
    flux_bot = [layers[x].dbot[:, 0:1] * (p[x][:, 0:1] - gbot[x]) for x in range(count)]
    flux_top = [layers[x].dtop[:, end:] * (p[x][:, end:] - gtop[x]) for x in range(count)]
    cbot_out[...] = traces(flux_bot, bot)
    ctop_out[...] = traces(flux_top, top)


def call(kernel, outs, args, scratch=()):
    return pl.pallas_call(
        kernel,
        out_shape=[jax.ShapeDtypeStruct(shape, F32) for shape in outs],
        in_specs=[VMEM] * len(args),
        out_specs=[VMEM] * len(outs),
        scratch_shapes=[pltpu.VMEM(shape, F32) for shape in scratch],
    )(*args)


def sub_swaps(blocks, subs):
    flat = lambda b, s: b * subs + s
    first = [(flat(b, s), flat(b, s ^ 1)) for b in range(blocks) for s in range(subs)]
    second = []
    for b in range(blocks):
        for s in range(subs):
            other = s + 1 if s % 2 else s - 1
            inside = 0 <= other < subs
            second.append((flat(b, s), flat(b, other) if inside else flat(b ^ 1, s)))
    return first, second


def shards(source, trans_x, trans_y, trans_z, mortar_bot, mortar_top):
    count, rows, cells = source.shape[1:]
    width = mortar_bot.shape[3]
    subs = lax.axis_size("sub")
    blocks = lax.axis_size("block")
    assert subs % 2 == 0 and blocks % 2 == 0 and count > HALO
    names = ("block", "sub")
    pair_one, pair_two = sub_swaps(blocks, subs)

    def trade(a, b):
        return lax.ppermute(a, names, pair_one), lax.ppermute(b, names, pair_two)

    coeffs = (source, trans_x, trans_y, trans_z)
    faces = (mortar_bot, mortar_top)
    face = (rows, cells)
    edges = call(edge_kernel, [(EDGE,) + face] * 2, coeffs)
    got = trade(*edges)
    moved = call(
        rest_kernel,
        [(REST,) + face] * 2 + [(2 * HALO, rows, width)] * 2,
        coeffs + faces,
    )
    more = trade(*moved[:2])
    more_rows = trade(*moved[2:])
    third, halo_a, halo_b, share_a, share_b = call(
        first_kernel,
        [(count,) + face] + [(HALO + 1,) + face] * 2 + [(1, width)] * 2,
        coeffs + faces + got,
        [(EDGE,) + face] * 2,
    )

    block_one = [(b, b ^ 1) for b in range(blocks)]
    block_two = [(b, (b + 1 if b % 2 else b - 1) % blocks) for b in range(blocks)]

    def everyone(value):
        if subs <= 4:
            swaps = range(subs - 1, 0, -1)
            return [value] + [
                lax.ppermute(value, "sub", [(i, i ^ k) for i in range(subs)]) for k in swaps
            ]
        return [lax.psum(value, "sub")]

    near_a = lax.ppermute(share_a, "block", block_one)
    near_b = lax.ppermute(share_b, "block", block_two)
    halos = trade(halo_a, halo_b)
    jumps = jnp.concatenate([share_a + near_a, share_b + near_b], axis=0)
    parts = everyone(jumps)
    pressure, cbot, ctop, mortar = call(
        second_kernel,
        [source.shape] + [(1, width)] * 3,
        coeffs + faces + got + tuple(more) + tuple(more_rows) + (third,) + halos + tuple(parts),
        [(EDGE,) + face] * 2
        + [(REST,) + face] * 2
        + [(2 * HALO, rows, width)] * 2
        + [(HALO + 1,) + face] * 2,
    )
    upper = lax.ppermute(cbot, "block", [((b + 1) % blocks, b) for b in range(blocks)])
    total = mortar + MORTAR_STEP * sum(everyone(ctop + upper))
    share = width // subs
    final = lax.dynamic_slice_in_dim(total[0], lax.axis_index("sub") * share, share, 0)
    return pressure, final[None]


def solution(mesh):
    spec = P("block", "sub", None, None)
    return jax.shard_map(
        shards,
        mesh=mesh,
        in_specs=(spec,) * 6,
        out_specs=(spec, P("block", "sub")),
        check_vma=False,
    )
```

time: 100 us -> 71.3 us (0.71)
  the two profiles are of different devices: /device:TPU:12 before, /device:TPU:0 now
where the time goes in v1:
time: 71.3 us; the launch traced here: 71.1 us
  starting transfers between devices  26.5 us (37%)
  waiting for transfers between devices  26.1 us (37%)
  Pallas kernels  13.6 us (19%)
  local copies, waits for them, and re-layouts  3.47 us (5%)
  between operations  0.79 us (1%)
    ppermute x6, waiting for transfers between devices, everyone(): lax.ppermute(value, 'sub', [(i, i ^ k) for i in range(subs)])  16.4 us
    ppermute x6, starting transfers between devices, everyone(): lax.ppermute(value, 'sub', [(i, i ^ k) for i in range(subs)])  15.2 us
    pallas_call x4, Pallas kernels, call(): pl.pallas_call(kernel, out_shape=[jax.ShapeDtypeStruct(shape, F32) for sh...  13.6 us
    ppermute x8, starting transfers between devices, trade(): return (lax.ppermute(a, names, pair_one), lax.ppermute(b, names, pair_two))  9 us
    ppermute x8, waiting for transfers between devices, trade(): return (lax.ppermute(a, names, pair_one), lax.ppermute(b, names, pair_two))  5.63 us
    unnamed x36, local copies, waits for them, and re-layouts  3.47 us
    ppermute x1, starting transfers between devices, shards(): near_b = lax.ppermute(share_b, 'block', block_two)  2.28 us
    ppermute x1, waiting for transfers between devices, shards(): near_b = lax.ppermute(share_b, 'block', block_two)  1.61 us
  transfers between devices with their start and end apart: 17, of which 10 were waited for; matrix products, arithmetic and copies ran while one was open for 0% of the time, Pallas kernels for 9%

profile of v1, /device:TPU:0, one launch (start us, length us, event | category | flops | bytes accessed | tf_op | source)
XLA Modules:
  0.0 71.1 jit_solution(4767034232747231264)
XLA Ops:
  0.6 2.3 %shard_map.77 = (f32[5,128,128]{2,1,0:T(8,128)}, f32[5,128,128]{2,1,0:T(8,128)}) custom-call(f32[1,4,128,128]{3,2,1,0:T(8,128)} %src.7, f32[1,4,128,128]{3,2,1,0:T(8,128)} %tx.7, f32[1,4,128,128]{3,2,1,0:T(8,128)} %ty.7, f32[1,4,128,128]{3,2,1,0:T(8,128)} %tz.7), custom_call_target="tpu_custom_call" | custom-call | tf_op jit(solution)/shard_map/pallas_call | solution.py:292
  2.9 3.1 %collective-permute-start = (f32[5,128,128]{2,1,0:T(8,128)}, f32[5,128,128]{2,1,0:T(8,128)S(1)}, u32[]{:S(2)}, u32[]{:S(2)}) collective-permute-start(f32[5,128,128]{2,1,0:T(8,128)} %get-tuple-element.17), channel_id=1, source_target_pairs={{0,1},{1,0},{2,3},{3,2},{4,5},{5,4},{6,7},{7,6},{8,9},{9,8},{10,11... | collective-permute-start | bytes 983048 | tf_op jit(solution)/shard_map/ppermute | solution.py:323
  6.0 3.0 %shard_map.78 = (f32[8,128,128]{2,1,0:T(8,128)}, f32[8,128,128]{2,1,0:T(8,128)}, f32[4,128,256]{2,1,0:T(8,128)}, f32[4,128,256]{2,1,0:T(8,128)}) custom-call(f32[1,4,128,128]{3,2,1,0:T(8,128)} %src.7, f32[1,4,128,128]{3,2,1,0:T(8,128)} %tx.7, f32[1,4,128,128]{3,2,1,0:T(8,128)} %ty.7, f32[1,4,128,128]{3,2,1,0:T(8,128)} %tz.7, f32[1,4,128,256]{3,2,1,0:T(8,128)} %bot.5, ...), custom_call_target="tpu_custom_call" | custom-call | tf_op jit(solution)/shard_map/pallas_call | solution.py:292
  9.5 3.5 %collective-permute-start.4 = (f32[4,128,256]{2,1,0:T(8,128)}, f32[4,128,256]{2,1,0:T(8,128)S(1)}, u32[]{:S(2)}, u32[]{:S(2)}) collective-permute-start(f32[4,128,256]{2,1,0:T(8,128)} %get-tuple-element.21), channel_id=1, source_target_pairs={{0,1},{1,0},{2,3},{3,2},{4,5},{5,4},{6,7},{7,6},{8,9},{9,8},{10,11... | collective-permute-start | bytes 1572872 | tf_op jit(solution)/shard_map/ppermute | solution.py:323
  13.0 1.7 %collective-permute-done.got_a = f32[5,128,128]{2,1,0:T(8,128)S(1)} collective-permute-done((f32[5,128,128]{2,1,0:T(8,128)}, f32[5,128,128]{2,1,0:T(8,128)S(1)}, u32[]{:S(2)}, u32[]{:S(2)}) %collective-permute-start) | collective-permute-done | bytes 327712 | tf_op jit(solution)/shard_map/ppermute | solution.py:323
  16.2 3.5 %shard_map.79 = (f32[4,128,128]{2,1,0:T(8,128)}, f32[3,128,128]{2,1,0:T(8,128)}, f32[3,128,128]{2,1,0:T(8,128)}, f32[1,256]{1,0:T(1,128)}, f32[1,256]{1,0:T(1,128)}) custom-call(f32[1,4,128,128]{3,2,1,0:T(8,128)} %src.7, f32[1,4,128,128]{3,2,1,0:T(8,128)} %tx.7, f32[1,4,128,128]{3,2,1,0:T(8,128)} %ty.7, f32[1,4,128,128]{3,2,1,0:T(8,128)} %tz.7, ...), custom_call_target="tpu_custom_call" | custom-call | tf_op jit(solution)/shard_map/pallas_call | solution.py:292
  20.3 2.3 %collective-permute-start.9 = (f32[1,256]{1,0:T(1,128)S(1)}, f32[1,256]{1,0:T(1,128)S(1)}, u32[]{:S(2)}, u32[]{:S(2)}) collective-permute-start(f32[1,256]{1,0:T(1,128)S(1)} %copy-done.14), channel_id=1, source_target_pairs={{0,28},{4,8},{8,4},{12,16},{16,12},{20,24},{24,20},{28,0},{1,29},{... | collective-permute-start | bytes 3080 | tf_op jit(solution)/shard_map/ppermute | solution.py:356
  22.6 1.6 %collective-permute-done.9 = f32[1,256]{1,0:T(1,128)S(1)} collective-permute-done((f32[1,256]{1,0:T(1,128)S(1)}, f32[1,256]{1,0:T(1,128)S(1)}, u32[]{:S(2)}, u32[]{:S(2)}) %collective-permute-start.9) | collective-permute-done | bytes 1056 | tf_op jit(solution)/shard_map/ppermute | solution.py:356
  24.2 1.2 %collective-permute-done.8 = f32[1,256]{1,0:T(1,128)S(1)} collective-permute-done((f32[1,256]{1,0:T(1,128)S(1)}, f32[1,256]{1,0:T(1,128)S(1)}, u32[]{:S(2)}, u32[]{:S(2)}) %collective-permute-start.8) | collective-permute-done | bytes 1056 | tf_op jit(solution)/shard_map/ppermute | solution.py:355
  25.4 4.1 %collective-permute-start.10 = (f32[2,256]{1,0:T(2,128)S(1)}, f32[2,256]{1,0:T(2,128)S(1)}, u32[]{:S(2)}, u32[]{:S(2)}) collective-permute-start(f32[2,256]{1,0:T(2,128)S(1)} %pad_maximum_fusion.rest_0_), channel_id=1, source_target_pairs={{0,3},{1,2},{2,1},{3,0},{4,7},{5,6},{6,5},{7,4},{8,11},{9,10},{10,... | collective-permute-start | bytes 6152 | tf_op jit(solution)/shard_map/ppermute | solution.py:351
  29.5 9.2 %collective-permute-done.10.rest_1_ = f32[2,256]{1,0:T(2,128)S(1)} collective-permute-done((f32[2,256]{1,0:T(2,128)S(1)}, f32[2,256]{1,0:T(2,128)S(1)}, u32[]{:S(2)}, u32[]{:S(2)}) %collective-permute-start.10) | collective-permute-done | bytes 2080 | tf_op jit(solution)/shard_map/ppermute | solution.py:351
  38.7 4.8 %collective-permute-start.11 = (f32[2,256]{1,0:T(2,128)S(1)}, f32[2,256]{1,0:T(2,128)S(1)}, u32[]{:S(2)}, u32[]{:S(2)}) collective-permute-start(f32[2,256]{1,0:T(2,128)S(1)} %pad_maximum_fusion.rest_0_), channel_id=1, source_target_pairs={{0,2},{1,3},{2,0},{3,1},{4,6},{5,7},{6,4},{7,5},{8,10},{9,11},{10,... | collective-permute-start | bytes 6152 | tf_op jit(solution)/shard_map/ppermute | solution.py:351
  43.5 1.6 %collective-permute-done.11.rest_2_ = f32[2,256]{1,0:T(2,128)S(1)} collective-permute-done((f32[2,256]{1,0:T(2,128)S(1)}, f32[2,256]{1,0:T(2,128)S(1)}, u32[]{:S(2)}, u32[]{:S(2)}) %collective-permute-start.11) | collective-permute-done | bytes 2080 | tf_op jit(solution)/shard_map/ppermute | solution.py:351
  45.0 1.9 %collective-permute-start.12 = (f32[2,256]{1,0:T(2,128)S(1)}, f32[2,256]{1,0:T(2,128)S(1)}, u32[]{:S(2)}, u32[]{:S(2)}) collective-permute-start(f32[2,256]{1,0:T(2,128)S(1)} %pad_maximum_fusion.rest_0_), channel_id=1, source_target_pairs={{0,1},{1,0},{2,3},{3,2},{4,5},{5,4},{6,7},{7,6},{8,9},{9,8},{10,11... | collective-permute-start | bytes 6152 | tf_op jit(solution)/shard_map/ppermute | solution.py:351
  46.9 1.7 %collective-permute-done.12.rest_3_ = f32[2,256]{1,0:T(2,128)S(1)} collective-permute-done((f32[2,256]{1,0:T(2,128)S(1)}, f32[2,256]{1,0:T(2,128)S(1)}, u32[]{:S(2)}, u32[]{:S(2)}) %collective-permute-start.12) | collective-permute-done | bytes 2080 | tf_op jit(solution)/shard_map/ppermute | solution.py:351
  48.6 1.9 %collective-permute-start.6 = (f32[3,128,128]{2,1,0:T(8,128)}, f32[3,128,128]{2,1,0:T(8,128)S(1)}, u32[]{:S(2)}, u32[]{:S(2)}) collective-permute-start(f32[3,128,128]{2,1,0:T(8,128)} %get-tuple-element.24), channel_id=1, source_target_pairs={{0,1},{1,0},{2,3},{3,2},{4,5},{5,4},{6,7},{7,6},{8,9},{9,8},{10,11... | collective-permute-start | bytes 589832 | tf_op jit(solution)/shard_map/ppermute | solution.py:323
  50.6 3.9 %collective-permute-done.6.halo_a = f32[3,128,128]{2,1,0:T(8,128)S(1)} collective-permute-done((f32[3,128,128]{2,1,0:T(8,128)}, f32[3,128,128]{2,1,0:T(8,128)S(1)}, u32[]{:S(2)}, u32[]{:S(2)}) %collective-permute-start.6) | collective-permute-done | bytes 196640 | tf_op jit(solution)/shard_map/ppermute | solution.py:323
  55.3 4.9 %shard_map.80 = (f32[1,4,128,128]{3,2,1,0:T(8,128)}, f32[1,256]{1,0:T(1,128)}, f32[1,256]{1,0:T(1,128)}, f32[1,256]{1,0:T(1,128)}) custom-call(f32[1,4,128,128]{3,2,1,0:T(8,128)} %src.7, f32[1,4,128,128]{3,2,1,0:T(8,128)} %tx.7, f32[1,4,128,128]{3,2,1,0:T(8,128)} %ty.7, f32[1,4,128,128]{3,2,1,0:T(8,128)} %tz.7, f32[1,4,128,256]{3,2,1,0:T(8,128)} %bot.5, ...), custom_call_target="tpu_custom_call" | custom-call | tf_op jit(solution)/shard_map/pallas_call | solution.py:292
  60.8 1.3 %collective-permute-done.13 = f32[1,256]{1,0:T(1,128)S(1)} collective-permute-done((f32[1,256]{1,0:T(1,128)S(1)}, f32[1,256]{1,0:T(1,128)S(1)}, u32[]{:S(2)}, u32[]{:S(2)}) %collective-permute-start.13) | collective-permute-done | bytes 1056 | tf_op jit(solution)/shard_map/ppermute | solution.py:369
  62.2 1.9 %collective-permute-start.16 = (f32[1,256]{1,0:T(1,128)S(1)}, f32[1,256]{1,0:T(1,128)S(1)}, u32[]{:S(2)}, u32[]{:S(2)}) collective-permute-start(f32[1,256]{1,0:T(1,128)S(1)} %add.26), channel_id=1, source_target_pairs={{0,1},{1,0},{2,3},{3,2},{4,5},{5,4},{6,7},{7,6},{8,9},{9,8},{10,11... | collective-permute-start | bytes 3080 | tf_op jit(solution)/shard_map/ppermute | solution.py:351
  64.1 1.0 %collective-permute-start.15 = (f32[1,256]{1,0:T(1,128)S(1)}, f32[1,256]{1,0:T(1,128)S(1)}, u32[]{:S(2)}, u32[]{:S(2)}) collective-permute-start(f32[1,256]{1,0:T(1,128)S(1)} %add.26), channel_id=1, source_target_pairs={{0,2},{1,3},{2,0},{3,1},{4,6},{5,7},{6,4},{7,5},{8,10},{9,11},{10,... | collective-permute-start | bytes 3080 | tf_op jit(solution)/shard_map/ppermute | solution.py:351
  65.1 1.4 %collective-permute-start.14 = (f32[1,256]{1,0:T(1,128)S(1)}, f32[1,256]{1,0:T(1,128)S(1)}, u32[]{:S(2)}, u32[]{:S(2)}) collective-permute-start(f32[1,256]{1,0:T(1,128)S(1)} %add.26), channel_id=1, source_target_pairs={{0,3},{1,2},{2,1},{3,0},{4,7},{5,6},{6,5},{7,4},{8,11},{9,10},{10,... | collective-permute-start | bytes 3080 | tf_op jit(solution)/shard_map/ppermute | solution.py:351
  66.5 2.0 %collective-permute-done.15 = f32[1,256]{1,0:T(1,128)S(1)} collective-permute-done((f32[1,256]{1,0:T(1,128)S(1)}, f32[1,256]{1,0:T(1,128)S(1)}, u32[]{:S(2)}, u32[]{:S(2)}) %collective-permute-start.15) | collective-permute-done | bytes 1056 | tf_op jit(solution)/shard_map/ppermute | solution.py:351
  68.6 1.9 %collective-permute-done.14 = f32[1,256]{1,0:T(1,128)S(1)} collective-permute-done((f32[1,256]{1,0:T(1,128)S(1)}, f32[1,256]{1,0:T(1,128)S(1)}, u32[]{:S(2)}, u32[]{:S(2)}) %collective-permute-start.14) | collective-permute-done | bytes 1056 | tf_op jit(solution)/shard_map/ppermute | solution.py:351
  (55 shorter events, 4.7 us)
Async XLA Ops:
  2.9 6.1 %copy-start.16 = (f32[5,128,128]{2,1,0:T(8,128)S(1)}, f32[5,128,128]{2,1,0:T(8,128)}, u32[]{:S(2)}) copy-start(f32[5,128,128]{2,1,0:T(8,128)} %get-tuple-element.18) | copy-start | bytes 983044
  2.9 11.8 %collective-permute-start = (f32[5,128,128]{2,1,0:T(8,128)}, f32[5,128,128]{2,1,0:T(8,128)S(1)}, u32[]{:S(2)}, u32[]{:S(2)}) collective-permute-start(f32[5,128,128]{2,1,0:T(8,128)} %get-tuple-element.17), channel_id=1, source_target_pairs={{0,1},{1,0},{2,3},{3,2},{4,5},{5,4},{6,7},{7,6},{8,9},{9,8},{10,11... | collective-permute-start | bytes 983048 | tf_op jit(solution)/shard_map/ppermute | solution.py:323
  9.0 41.6 %collective-permute-start.2 = (f32[8,128,128]{2,1,0:T(8,128)}, f32[8,128,128]{2,1,0:T(8,128)S(1)}, u32[]{:S(2)}, u32[]{:S(2)}) collective-permute-start(f32[8,128,128]{2,1,0:T(8,128)} %get-tuple-element.19), channel_id=1, source_target_pairs={{0,1},{1,0},{2,3},{3,2},{4,5},{5,4},{6,7},{7,6},{8,9},{9,8},{10,11... | collective-permute-start | bytes 1572872 | tf_op jit(solution)/shard_map/ppermute | solution.py:323
  9.0 5.7 %collective-permute-start.1 = (f32[5,128,128]{2,1,0:T(8,128)S(1)}, f32[5,128,128]{2,1,0:T(8,128)S(1)}, u32[]{:S(2)}, u32[]{:S(2)}) collective-permute-start(f32[5,128,128]{2,1,0:T(8,128)S(1)} %copy-done.16), channel_id=1, source_target_pairs={{0,4},{1,2},{2,1},{3,7},{4,0},{5,6},{6,5},{7,3},{8,12},{9,10},{10,... | collective-permute-start | bytes 983048 | tf_op jit(solution)/shard_map/ppermute | solution.py:323
  9.0 41.5 %collective-permute-start.3 = (f32[8,128,128]{2,1,0:T(8,128)}, f32[8,128,128]{2,1,0:T(8,128)S(1)}, u32[]{:S(2)}, u32[]{:S(2)}) collective-permute-start(f32[8,128,128]{2,1,0:T(8,128)} %get-tuple-element.20), channel_id=1, source_target_pairs={{0,4},{1,2},{2,1},{3,7},{4,0},{5,6},{6,5},{7,3},{8,12},{9,10},{10,... | collective-permute-start | bytes 1572872 | tf_op jit(solution)/shard_map/ppermute | solution.py:323
  9.5 41.0 %collective-permute-start.4 = (f32[4,128,256]{2,1,0:T(8,128)}, f32[4,128,256]{2,1,0:T(8,128)S(1)}, u32[]{:S(2)}, u32[]{:S(2)}) collective-permute-start(f32[4,128,256]{2,1,0:T(8,128)} %get-tuple-element.21), channel_id=1, source_target_pairs={{0,1},{1,0},{2,3},{3,2},{4,5},{5,4},{6,7},{7,6},{8,9},{9,8},{10,11... | collective-permute-start | bytes 1572872 | tf_op jit(solution)/shard_map/ppermute | solution.py:323
  14.7 35.9 %collective-permute-start.5 = (f32[4,128,256]{2,1,0:T(8,128)}, f32[4,128,256]{2,1,0:T(8,128)S(1)}, u32[]{:S(2)}, u32[]{:S(2)}) collective-permute-start(f32[4,128,256]{2,1,0:T(8,128)} %get-tuple-element.22), channel_id=1, source_target_pairs={{0,4},{1,2},{2,1},{3,7},{4,0},{5,6},{6,5},{7,3},{8,12},{9,10},{10,... | collective-permute-start | bytes 1572872 | tf_op jit(solution)/shard_map/ppermute | solution.py:323
  20.3 3.9 %collective-permute-start.9 = (f32[1,256]{1,0:T(1,128)S(1)}, f32[1,256]{1,0:T(1,128)S(1)}, u32[]{:S(2)}, u32[]{:S(2)}) collective-permute-start(f32[1,256]{1,0:T(1,128)S(1)} %copy-done.14), channel_id=1, source_target_pairs={{0,28},{4,8},{8,4},{12,16},{16,12},{20,24},{24,20},{28,0},{1,29},{... | collective-permute-start | bytes 3080 | tf_op jit(solution)/shard_map/ppermute | solution.py:356
  24.2 1.2 %collective-permute-start.8 = (f32[1,256]{1,0:T(1,128)S(1)}, f32[1,256]{1,0:T(1,128)S(1)}, u32[]{:S(2)}, u32[]{:S(2)}) collective-permute-start(f32[1,256]{1,0:T(1,128)S(1)} %copy-done.13), channel_id=1, source_target_pairs={{0,4},{4,0},{8,12},{12,8},{16,20},{20,16},{24,28},{28,24},{1,5},{5... | collective-permute-start | bytes 3080 | tf_op jit(solution)/shard_map/ppermute | solution.py:355
  25.4 29.1 %copy-start.8 = (f32[2,256]{1,0:T(2,128)}, f32[2,256]{1,0:T(2,128)S(1)}, u32[]{:S(2)}) copy-start(f32[2,256]{1,0:T(2,128)S(1)} %pad_maximum_fusion.rest_0_) | copy-start | bytes 6148
  25.4 13.3 %collective-permute-start.10 = (f32[2,256]{1,0:T(2,128)S(1)}, f32[2,256]{1,0:T(2,128)S(1)}, u32[]{:S(2)}, u32[]{:S(2)}) collective-permute-start(f32[2,256]{1,0:T(2,128)S(1)} %pad_maximum_fusion.rest_0_), channel_id=1, source_target_pairs={{0,3},{1,2},{2,1},{3,0},{4,7},{5,6},{6,5},{7,4},{8,11},{9,10},{10,... | collective-permute-start | bytes 6152 | tf_op jit(solution)/shard_map/ppermute | solution.py:351
  38.7 15.9 %copy-start.9 = (f32[2,256]{1,0:T(2,128)}, f32[2,256]{1,0:T(2,128)S(1)}, u32[]{:S(2)}) copy-start(f32[2,256]{1,0:T(2,128)S(1)} %collective-permute-done.10.rest_1_) | copy-start | bytes 6148
  38.7 6.3 %collective-permute-start.11 = (f32[2,256]{1,0:T(2,128)S(1)}, f32[2,256]{1,0:T(2,128)S(1)}, u32[]{:S(2)}, u32[]{:S(2)}) collective-permute-start(f32[2,256]{1,0:T(2,128)S(1)} %pad_maximum_fusion.rest_0_), channel_id=1, source_target_pairs={{0,2},{1,3},{2,0},{3,1},{4,6},{5,7},{6,4},{7,5},{8,10},{9,11},{10,... | collective-permute-start | bytes 6152 | tf_op jit(solution)/shard_map/ppermute | solution.py:351
  45.0 9.5 %copy-start.10 = (f32[2,256]{1,0:T(2,128)}, f32[2,256]{1,0:T(2,128)S(1)}, u32[]{:S(2)}) copy-start(f32[2,256]{1,0:T(2,128)S(1)} %collective-permute-done.11.rest_2_) | copy-start | bytes 6148
  45.0 3.6 %collective-permute-start.12 = (f32[2,256]{1,0:T(2,128)S(1)}, f32[2,256]{1,0:T(2,128)S(1)}, u32[]{:S(2)}, u32[]{:S(2)}) collective-permute-start(f32[2,256]{1,0:T(2,128)S(1)} %pad_maximum_fusion.rest_0_), channel_id=1, source_target_pairs={{0,1},{1,0},{2,3},{3,2},{4,5},{5,4},{6,7},{7,6},{8,9},{9,8},{10,11... | collective-permute-start | bytes 6152 | tf_op jit(solution)/shard_map/ppermute | solution.py:351
  48.6 5.9 %copy-start.11 = (f32[2,256]{1,0:T(2,128)}, f32[2,256]{1,0:T(2,128)S(1)}, u32[]{:S(2)}) copy-start(f32[2,256]{1,0:T(2,128)S(1)} %collective-permute-done.12.rest_3_) | copy-start | bytes 6148
  48.6 5.9 %collective-permute-start.6 = (f32[3,128,128]{2,1,0:T(8,128)}, f32[3,128,128]{2,1,0:T(8,128)S(1)}, u32[]{:S(2)}, u32[]{:S(2)}) collective-permute-start(f32[3,128,128]{2,1,0:T(8,128)} %get-tuple-element.24), channel_id=1, source_target_pairs={{0,1},{1,0},{2,3},{3,2},{4,5},{5,4},{6,7},{7,6},{8,9},{9,8},{10,11... | collective-permute-start | bytes 589832 | tf_op jit(solution)/shard_map/ppermute | solution.py:323
  50.5 4.0 %copy-start.2 = (f32[8,128,128]{2,1,0:T(8,128)}, f32[8,128,128]{2,1,0:T(8,128)S(1)}, u32[]{:S(2)}) copy-start(f32[8,128,128]{2,1,0:T(8,128)S(1)} %collective-permute-done.2.rest_a) | copy-start | bytes 1572868
  50.5 4.0 %collective-permute-start.7 = (f32[3,128,128]{2,1,0:T(8,128)}, f32[3,128,128]{2,1,0:T(8,128)S(1)}, u32[]{:S(2)}, u32[]{:S(2)}) collective-permute-start(f32[3,128,128]{2,1,0:T(8,128)} %get-tuple-element.25), channel_id=1, source_target_pairs={{0,4},{1,2},{2,1},{3,7},{4,0},{5,6},{6,5},{7,3},{8,12},{9,10},{10,... | collective-permute-start | bytes 589832 | tf_op jit(solution)/shard_map/ppermute | solution.py:323
  50.5 4.0 %copy-start.3 = (f32[8,128,128]{2,1,0:T(8,128)}, f32[8,128,128]{2,1,0:T(8,128)S(1)}, u32[]{:S(2)}) copy-start(f32[8,128,128]{2,1,0:T(8,128)S(1)} %collective-permute-done.3.rest_b) | copy-start | bytes 1572868
  60.8 1.3 %collective-permute-start.13 = (f32[1,256]{1,0:T(1,128)S(1)}, f32[1,256]{1,0:T(1,128)S(1)}, u32[]{:S(2)}, u32[]{:S(2)}) collective-permute-start(f32[1,256]{1,0:T(1,128)S(1)} %copy-done.17), channel_id=1, source_target_pairs={{4,0},{8,4},{12,8},{16,12},{20,16},{24,20},{28,24},{0,28},{5,1},{9... | collective-permute-start | bytes 3080 | tf_op jit(solution)/shard_map/ppermute | solution.py:369
  62.2 4.4 %collective-permute-start.16 = (f32[1,256]{1,0:T(1,128)S(1)}, f32[1,256]{1,0:T(1,128)S(1)}, u32[]{:S(2)}, u32[]{:S(2)}) collective-permute-start(f32[1,256]{1,0:T(1,128)S(1)} %add.26), channel_id=1, source_target_pairs={{0,1},{1,0},{2,3},{3,2},{4,5},{5,4},{6,7},{7,6},{8,9},{9,8},{10,11... | collective-permute-start | bytes 3080 | tf_op jit(solution)/shard_map/ppermute | solution.py:351
  64.1 4.5 %collective-permute-start.15 = (f32[1,256]{1,0:T(1,128)S(1)}, f32[1,256]{1,0:T(1,128)S(1)}, u32[]{:S(2)}, u32[]{:S(2)}) collective-permute-start(f32[1,256]{1,0:T(1,128)S(1)} %add.26), channel_id=1, source_target_pairs={{0,2},{1,3},{2,0},{3,1},{4,6},{5,7},{6,4},{7,5},{8,10},{9,11},{10,... | collective-permute-start | bytes 3080 | tf_op jit(solution)/shard_map/ppermute | solution.py:351
  65.1 5.4 %collective-permute-start.14 = (f32[1,256]{1,0:T(1,128)S(1)}, f32[1,256]{1,0:T(1,128)S(1)}, u32[]{:S(2)}, u32[]{:S(2)}) collective-permute-start(f32[1,256]{1,0:T(1,128)S(1)} %add.26), channel_id=1, source_target_pairs={{0,3},{1,2},{2,1},{3,0},{4,7},{5,6},{6,5},{7,4},{8,11},{9,10},{10,... | collective-permute-start | bytes 3080 | tf_op jit(solution)/shard_map/ppermute | solution.py:351
  (11 other events, 21.4 us)
